TPU v7x, 256 devices: a whole 4x4x8 slice. The times are simulated.
256 devices in a mesh: pair: 32 (over x, y, core), slab: 8 (over z).
Axes of the slice: x: 4, y: 4, z: 8, core: 2. Of those that a mesh axis runs over, the one named last changes fastest.
Arguments:
- amplitudes: bfloat16 [6144, 9216], P('pair', 'slab'), may hold values from -6 to 6
- integrals: bfloat16 [9216, 9216], P('slab', 'pair'), may hold values from -0.125 to 0.125
- pair_index: int32 [6144, 2], P('pair'), may hold values from 0 to 159, as said below
- eps_occ: float32 [160], replicated, may hold values from -2 to -0.5
- eps_vir: float32 [96], replicated, may hold values from 0.5 to 3
Outputs:
- update: float32 [6144, 9216], P('pair', 'slab')
Inputs may be any that keep to these rules, and one draw needn't show every extreme that they name: `pair_index`: each row holds i < j; pairs may repeat; pair 0 is (0, 159).
All inputs are finite; a program needn't handle non-finite values.
Results may differ from a plain program's by a relative error of at most 0.0003.
Values may be sent and summed in bfloat16 or wider, within the bound.
A program may use at most 128 MiB of HBM per device.

v0:
```python
import jax
import jax.numpy as jnp
from jax import lax
from jax.sharding import PartitionSpec as P


def on_device(amplitudes, integrals, pair_index, eps_occ, eps_vir):
    num_pairs = amplitudes.shape[0]
    vir_count = eps_vir.shape[0]
    ladder = jnp.dot(
        amplitudes,
        lax.all_gather(integrals, "pair", axis=1, tiled=True),
        preferred_element_type=jnp.float32,
    )
    ladder_cube = ladder.reshape(num_pairs, vir_count, vir_count)
    antisym = (ladder_cube - jnp.swapaxes(ladder_cube, 1, 2)).reshape(
        num_pairs, vir_count * vir_count
    )
    summed = lax.psum_scatter(antisym, "slab", scatter_dimension=1, tiled=True)
    col_count = summed.shape[1]
    column_ids = lax.axis_index("slab") * col_count + jnp.arange(col_count, dtype=jnp.int32)
    vir_ids = jnp.arange(vir_count, dtype=jnp.int32)
    eps_first = jnp.sum(
        jnp.where((column_ids // vir_count)[:, None] == vir_ids[None, :], eps_vir[None, :], 0.0),
        axis=1,
    )
    eps_second = jnp.sum(
        jnp.where((column_ids % vir_count)[:, None] == vir_ids[None, :], eps_vir[None, :], 0.0),
        axis=1,
    )
    occ_ids = jnp.arange(eps_occ.shape[0], dtype=jnp.int32)
    eps_iocc = jnp.sum(
        jnp.where(pair_index[:, 0:1] == occ_ids[None, :], eps_occ[None, :], 0.0), axis=1
    )
    eps_jocc = jnp.sum(
        jnp.where(pair_index[:, 1:2] == occ_ids[None, :], eps_occ[None, :], 0.0), axis=1
    )
    denominator = (eps_iocc + eps_jocc)[:, None] - (eps_first + eps_second)[None, :]
    return summed / denominator


def solution(mesh):
    in_specs = (P("pair", "slab"), P("slab", "pair"), P("pair", None), P(), P())
    out_specs = P("pair", "slab")
    return jax.shard_map(
        on_device, mesh=mesh, in_specs=in_specs, out_specs=out_specs, check_vma=False
    )
```

profile of v0, /device:TPU:1, one launch (start us, length us, event | category | flops | bytes accessed | tf_op | source)
XLA Modules:
  0.0 247.2 jit_solution(8957714024740094962)
XLA Ops:
  6.5 0.0 copy-start
  6.5 0.0 all-gather.2.cloned.1.call-start
  6.5 0.7 all-gather.2.cloned.1.call-update
  7.3 0.0 reduce-scatter.2.cloned.1.call-start
  7.3 94.7 %all-gather.2.cloned.1.call-done = bf16[1152,9216]{0,1:T(8,128)(2,1)} async-done(((bf16[1152,288]{0,1:T(8,128)(2,1)}), bf16[1152,9216]{0,1:T(8,128)(2,1)}) %all-gather.2.cloned.1.call-update) | async-done | bytes 21233680 | tf_op jit(solution)/shard_map/all_gather | solution.py:12
  102.0 0.0 copy-done
  102.0 13.1 %fusion.6 = f32[192,9216]{1,0:T(8,128)} fusion(bf16[192,1152]{1,0:T(8,128)(2,1)S(1)} %copy-done, bf16[1152,9216]{0,1:T(8,128)(2,1)} %all-gather.2.cloned.1.call-done), kind=kOutput, calls=%fused_computation.20 | convolution fusion | flops 4076863488 | bytes 28753920 | tf_op jit(solution)/shard_map/dot_general | solution.py:10
  115.1 9.3 %reshape.36 = f32[192,96,96]{2,1,0:T(8,128)} reshape(f32[192,9216]{1,0:T(8,128)} %fusion.6) | data formatting | bytes 14155776 | tf_op jit(solution)/shard_map/reshape | solution.py:15
  124.5 9.6 %copy.7 = f32[192,96,96]{1,2,0:T(8,128)} copy(f32[192,96,96]{2,1,0:T(8,128)} %reshape.36) | data formatting | bytes 14155776 | tf_op jit(solution)/shard_map/reshape | solution.py:15
  134.1 12.2 %bitcast_subtract_fusion = f32[192,96,96]{2,1,0:T(8,128)} fusion(f32[192,96,96]{2,1,0:T(8,128)} %reshape.36, f32[192,96,96]{1,2,0:T(8,128)} %copy.7), kind=kLoop, calls=%fused_computation | loop fusion | flops 1769472 | bytes 21233664 | tf_op jit(solution)/shard_map/sub | solution.py:16
  146.2 0.0 copy-start.3
  146.2 0.0 copy-start.1
  146.3 0.0 copy-start.2
  146.3 10.1 %reshape.37 = f32[192,9216]{1,0:T(8,128)} reshape(f32[192,96,96]{2,1,0:T(8,128)} %bitcast_subtract_fusion) | data formatting | bytes 14155776 | tf_op jit(solution)/shard_map/reshape | solution.py:16
  156.3 0.0 reduce-scatter.2.cloned.1.call-update
  156.4 0.0 copy-done.3
  156.4 0.2 select_reduce_fusion
  156.6 0.0 copy-done.1
  156.6 0.0 copy-done.2
  156.6 0.1 select_reduce_fusion.2
  156.8 81.3 %reduce-scatter.2.cloned.1.call-done = f32[192,1152]{1,0:T(8,128)} async-done(((f32[192,9216]{1,0:T(8,128)}), f32[192,1152]{1,0:T(8,128)}) %reduce-scatter.2.cloned.1.call-update) | async-done | bytes 884752 | tf_op jit(solution)/shard_map/reduce_scatter | solution.py:19
  238.1 2.3 subtract_divide_fusion
  (4 shorter events, 0.0 us)
Async XLA Ops:
  6.5 95.5 %copy-start = (bf16[192,1152]{1,0:T(8,128)(2,1)S(1)}, bf16[192,1152]{1,0:T(8,128)(2,1)}, u32[]{:S(2)}) copy-start(bf16[192,1152]{1,0:T(8,128)(2,1)} %param.5) | copy-start | bytes 1327108
  6.5 95.5 %all-gather.2.cloned.1.call-start = ((), (), s32[]{:S(2)}) async-start(), calls=%async_computation.1 | async-start | bytes 21897216 | tf_op jit(solution)/shard_map/all_gather | solution.py:12
  7.3 230.8 %reduce-scatter.2.cloned.1.call-start = ((), (), s32[]{:S(2)}) async-start(), calls=%async_computation.2 | async-start | bytes 7962624 | tf_op jit(solution)/shard_map/reduce_scatter | solution.py:19
  146.2 10.1 %copy-start.3 = (f32[96]{0:T(128)S(1)}, f32[96]{0:T(128)}, u32[]{:S(2)}) copy-start(f32[96]{0:T(128)} %param.9) | copy-start | bytes 1156
  146.2 10.4 %copy-start.1 = (s32[192,2]{0,1:T(2,128)S(1)}, s32[192,2]{0,1:T(2,128)}, u32[]{:S(2)}) copy-start(s32[192,2]{0,1:T(2,128)} %param.7) | copy-start | bytes 4612
  146.3 10.4 %copy-start.2 = (f32[160]{0:T(256)S(1)}, f32[160]{0:T(256)}, u32[]{:S(2)}) copy-start(f32[160]{0:T(256)} %param.8) | copy-start | bytes 1924
Sparse Core Ops, SparseCore 0:
  9.9 92.0 all-gather.1
  156.5 81.5 reduce-scatter.1
where the time goes:
time: 248 us; the launch traced here: 247 us
  waiting for transfers between devices  177 us (71%)
  local copies, waits for them, and re-layouts  29 us (12%)
  other arithmetic  14.8 us (6%)
  between operations  13.5 us (5%)
  matrix products  13.1 us (5%)
    all_gather x1, waiting for transfers between devices, on_device(): lax.all_gather(integrals, 'pair', axis=1, tiled=True)  94.7 us
    reduce_scatter x1, waiting for transfers between devices, on_device(): summed = lax.psum_scatter(antisym, 'slab', scatter_dimension=1, tiled=True)  81.3 us
    reshape x2, local copies, waits for them, and re-layouts, on_device(): ladder_cube = ladder.reshape(num_pairs, vir_count, vir_count)  18.9 us
    dot_general x1, matrix products, on_device(): jnp.dot(amplitudes, lax.all_gather(integrals, 'pair', axis=1, tiled=True)...  13.1 us
    sub x1, other arithmetic, on_device(): ladder_cube - jnp.swapaxes(ladder_cube, 1, 2)  12.2 us
    reshape x1, local copies, waits for them, and re-layouts, on_device(): (ladder_cube - jnp.swapaxes(ladder_cube, 1, 2)).reshape(num_pairs, vir_co...  10.1 us
  transfers between devices with their start and end apart: 2, of which 2 were waited for; matrix products, arithmetic and copies ran while one was open for 0% of the time, Pallas kernels for 0%

commit v1 on v0

v1 whole, which is shorter than its diff:
```python
import functools

import jax
import jax.numpy as jnp
import numpy as np
from jax import lax
from jax.experimental import pallas as pl
from jax.experimental.pallas import tpu as pltpu
from jax.sharding import PartitionSpec as P

MESH = pl.DeviceIdType.MESH
G = 12
BLOCK = (24, 16)
OWN = (48, 24)
QMAX = 32767.0


def chunk_of(u, v):
    return 0 if (u + v) % 3 else 1


def block_row(u, v):
    q = chunk_of(u, v)
    rank = sum(chunk_of(u, i) == q for i in range(v))
    return BLOCK[q] * (u // 3) + (8, 4)[q] * (u % 3) + rank


def own_row(i, v):
    q = chunk_of(i, v)
    return (8, 4)[q] * i + sum(chunk_of(i, j) == q for j in range(v))


def selection_tables():
    sel = [np.zeros((3, 2, OWN[q], 4 * BLOCK[q]), np.float32) for q in range(2)]
    for kind in range(3):
        for i in range(6):
            for v in range(G):
                u, vv = i, v
                if kind == 1:
                    u = i + 6
                if kind == 2 and v < i:
                    u, vv = i + 6, v + 6
                q = chunk_of(i, v)
                sel[q][kind, 0, own_row(i, v), block_row(u, vv)] = 1
                sel[q][kind, 1, own_row(i, v), block_row(vv, u)] = 1
    return sel


def output_tables():
    table = np.zeros((8, 4, G * 8 * G), np.int32)
    for w in range(8):
        for a in range(G):
            for o in range(8):
                for b in range(G):
                    col = (a * 8 + o) * G + b
                    if o > w:
                        u, v, s, h = a, b, 1, a // 6
                    elif o < w:
                        u, v, s, h = b, a, -1, b // 6
                    else:
                        lo, hi, s, h = min(a, b), max(a, b), (0 if a == b else 1 if a < b else -1), 0
                        if lo >= 6:
                            u, v, s = hi - 6, lo - 6, -s
                        else:
                            u, v = lo, hi
                    q = chunk_of(u, v)
                    row = 16 * OWN[0] * q + (o * 2 + h) * OWN[q] + own_row(u % 6, v)
                    table[w, :, col] = row, w * G + a, o * G + b, s
    return table


def row_order():
    order = np.zeros((8 * sum(BLOCK), 3 * 8 * G), np.float32)
    for o in range(8):
        for a in range(3):
            for b in range(G):
                q = chunk_of(a, b)
                order[8 * BLOCK[0] * q + o * BLOCK[q] + block_row(a, b), (a * 8 + o) * G + b] = 1
    return order


def xor3(a, b):
    out = 0
    for bit in (1, 2, 4):
        out = out + bit * lax.rem(lax.div(a, bit) + lax.div(b, bit), 2)
    return out


def quantize(val, q_ref, s_ref):
    r, width = val.shape
    cube = val.reshape(r // 8, 8, width)
    top = jnp.max(jnp.abs(cube), axis=0)
    top = functools.reduce(jnp.maximum, [top[:, 128 * i : 128 * (i + 1)] for i in range(width // 128)])
    top = jnp.maximum(top * (1.01 / QMAX), 1e-36).astype(jnp.bfloat16)
    inv = 1.0 / top.astype(jnp.float32)
    q = (cube * jnp.concatenate([inv] * (width // 128), axis=1) + 32768.5).astype(jnp.int32) - 32768
    q_ref[...] = q.reshape(r, width).astype(jnp.int16)
    s_ref[...] = top


def dequantize(q, s):
    r, width = q.shape
    cube = q.astype(jnp.int32).astype(jnp.float32).reshape(r // 8, 8, width)
    return (cube * jnp.concatenate([s.astype(jnp.float32)] * (width // 128), axis=1)).reshape(r, width)


def column(row):
    n = row.shape[1]
    same = lax.broadcasted_iota(jnp.int32, (n, n), 0) == lax.broadcasted_iota(jnp.int32, (n, n), 1)
    return jnp.sum(jnp.where(same, row, 0.0), axis=1, keepdims=True)


def looked_up(ids, table):
    hit = lax.broadcasted_iota(jnp.int32, (table.shape[0], ids.shape[1]), 0) == ids
    return jnp.sum(jnp.where(hit, table, 0.0), axis=0, keepdims=True)


def kernel(sel0_hbm, sel1_hbm, order_hbm, table_hbm, a_hbm, vt_hbm, pairs_hbm, occ_hbm, vir_hbm, out_hbm,
           sel0, sel1, order_ref, table_ref, vt_ref, pairs_ref, occ_ref, vir_ref, in_s, out_s, out_ref,
           a_all, w_ref, o_ref, ep_ref, ev_ref,
           vl0, vl1, vb0, vb1, va0, va1, vc0, vc1, cs0, cs1, rq0, rq1, sq0, sq1, fq0, fq1, gq0, gq1,
           rs, ss, fs, gs,
           vx_s, vx_r, vy_s, vy_r, vf_s, vf_r, ax_s, ax_r, af_s, af_r, ap_s, ap_r, own_s,
           rq_s, rq_r, rs_s, rs_r, fq_s, fq_r, fs_s, fs_r):
    sel, v_local, v_buf, v_one, v_two, cs = (sel0, sel1), (vl0, vl1), (vb0, vb1), (va0, va1), (vc0, vc1), (cs0, cs1)
    rq, sq, fq, gq = (rq0, rq1), (sq0, sq1), (fq0, fq1), (gq0, gq1)
    pair, z = lax.axis_index("pair"), lax.axis_index("slab")
    x, y, c = lax.div(pair, 8), lax.rem(lax.div(pair, 2), 4), lax.rem(pair, 2)

    def kid(xx, cc):
        return xx + 4 * cc

    kappa = kid(x, c)
    w_mine = lax.div(pair, 4)

    def dev(xx, yy, cc, zz):
        return ((xx * 4 + yy) * 2 + cc, zz)

    def step(i, d, n):
        return lax.rem(i + d + n, n)

    def remote(src, dst, ssem, rsem, to):
        return pltpu.make_async_remote_copy(
            src_ref=src, dst_ref=dst, send_sem=ssem, recv_sem=rsem, device_id=to, device_id_type=MESH
        )

    other = dev(x, y, 1 - c, z)
    a_ref = a_all.at[x, c]
    inputs = [
        pltpu.make_async_copy(src, dst, in_s.at[i])
        for i, (src, dst) in enumerate(
            (
                (order_hbm, order_ref), (vt_hbm, vt_ref), (a_hbm, a_ref), (table_hbm, table_ref), (sel0_hbm, sel0),
                (sel1_hbm, sel1), (pairs_hbm, pairs_ref), (occ_hbm, occ_ref), (vir_hbm, vir_ref),
            )
        )
    ]
    for cp in inputs:
        cp.start()

    barrier = pltpu.get_barrier_semaphore()

    def greet(to):
        pl.semaphore_signal(barrier, inc=1, device_id=to, device_id_type=MESH)

    for dx in range(4):
        for dc in range(2):
            if dx or dc:
                greet(dev(step(x, dx, 4), y, step(c, dc, 2), z))
    for d in (1, -1):
        greet(dev(x, step(y, d, 4), c, z))
        greet(dev(x, y, c, step(z, d, 8)))
    inputs[0].wait()
    inputs[1].wait()
    ordered = jnp.dot(order_ref[...], vt_ref[...], preferred_element_type=jnp.float32).astype(jnp.bfloat16)
    v_local[0][...] = ordered[: 8 * BLOCK[0]].reshape(v_local[0].shape)
    v_local[1][...] = ordered[8 * BLOCK[0] :].reshape(v_local[1].shape)
    pl.semaphore_wait(barrier, 11)

    slot_y = lax.rem(y, 2) * 2
    ring = (0, 1, 3, 2)

    def to_class(q, dx, dc):
        xx, cc = step(x, dx, 4), step(c, dc, 2)
        src = v_local[q].at[xor3(w_mine, kid(xx, cc))]
        dst = v_buf[q].at[w_mine, slot_y + c]
        if dx or dc:
            return remote(src, dst, vx_s.at[q, dx * 2 + dc], vx_r.at[q, kappa], dev(xx, y, cc, z))
        return pltpu.make_async_copy(src, dst, own_s.at[0, q])

    for q in range(2):
        for dx in (1, 3, 2, 0):
            for dc in (0, 1):
                to_class(q, dx, dc).start()
    inputs[2].wait()
    for h in range(2):
        for d, di in ((1, 0), (-1, 1)):
            hh = h if di == 0 else 1 - h
            part = a_all.at[x, c, pl.ds(96 * hh, 96)]
            remote(part, part, ax_s.at[di, hh], ax_r.at[di, hh], dev(step(x, d, 4), y, c, z)).start()
    remote(a_ref, a_ref, ap_s.at[0], ap_r.at[0], other).start()

    def v_slot(q, yy, xx, cc):
        return v_buf[q].at[2 * xx + lax.div(yy, 2), lax.rem(yy, 2) * 2 + cc]

    def to_y(d):
        return dev(x, step(y, d, 4), c, z)

    def spread(q):
        for dx in ring:
            for dc in range(2):
                xx, cc = step(x, dx, 4), step(c, dc, 2)
                blk = v_slot(q, y, xx, cc)
                if dx or dc:
                    remote(blk, blk, vx_s.at[q, 0], vx_r.at[q, kid(xx, cc)], other).wait_recv()
                else:
                    to_class(q, 0, 0).wait()
                for d, di in ((1, 0), (-1, 1)):
                    u = dx * 2 + cc
                    remote(blk, blk, vy_s.at[q, di, u], vy_r.at[q, di, u], to_y(d)).start()

    def pass_on(q):
        for dx in ring:
            for d, di in ((1, 0), (-1, 1)):
                u = dx * 2 + di
                blk = v_slot(q, step(y, -d, 4), step(x, dx, 4), di)
                remote(blk, blk, vy_s.at[q, di, u], vy_r.at[q, di, u], other).wait_recv()
                remote(blk, blk, vf_s.at[q, u], vf_r.at[q, u], to_y(d)).start()

    def gathered(q):
        for d, di in ((1, 0), (-1, 1)):
            for dx in ring:
                u = dx * 2 + 1 - di
                blk = v_slot(q, step(y, -d, 4), step(x, dx, 4), 1 - di)
                remote(blk, blk, vy_s.at[q, di, u], vy_r.at[q, di, u], other).wait_recv()
        for dx in ring:
            for di in range(2):
                u = dx * 2 + di
                blk = v_slot(q, step(y, 2, 4), step(x, dx, 4), di)
                remote(blk, blk, vf_s.at[q, u], vf_r.at[q, u], other).wait_recv()

    def pass_on_a():
        for d, di in ((1, 0), (-1, 1)):
            blk = a_all.at[step(x, -d, 4), c, pl.ds(96 * di, 96)]
            remote(blk, blk, ax_s.at[di, di], ax_r.at[di, di], other).wait_recv()
            remote(blk, blk, af_s.at[di], af_r.at[di], dev(step(x, d, 4), y, c, z)).start()

    def share_near():
        for n, d, di in ((1, 1, 0), (2, -1, 1)):
            blk = a_all.at[step(x, -d, 4), c]
            part = a_all.at[step(x, -d, 4), c, pl.ds(96 * (1 - di), 96)]
            remote(part, part, ax_s.at[di, 1 - di], ax_r.at[di, 1 - di], other).wait_recv()
            remote(blk, blk, ap_s.at[n], ap_r.at[n], other).start()

    def share_far():
        far = a_all.at[step(x, 2, 4), c]
        for di in range(2):
            part = a_all.at[step(x, 2, 4), c, pl.ds(96 * di, 96)]
            remote(part, part, af_s.at[di], af_r.at[di], other).wait_recv()
        remote(far, far, ap_s.at[3], ap_r.at[3], other).start()

    def other_core(n, dx):
        blk = a_all.at[step(x, dx, 4), 1 - c]
        remote(blk, blk, ap_s.at[n], ap_r.at[n], other).wait_recv()

    targets = (4, 3, -3, 2, -2, 1, -1, 0)

    def select(q, first, last):
        for j in range(first, last):
            t = step(z, targets[j], 8)
            o = xor3(t, kappa)
            lo, hi = jnp.minimum(t, o), jnp.maximum(t, o)
            kind = jnp.where(kappa == 0, 2, jnp.where(t == lo, 0, 1))
            rows = pl.ds(j * OWN[q], OWN[q])
            for i, (dst, w) in enumerate(((v_one[q], lo), (v_two[q], hi))):
                dst[rows, :] = jnp.dot(
                    sel[q][kind, i], v_buf[q][w].reshape(4 * BLOCK[q], -1), preferred_element_type=jnp.float32
                ).astype(jnp.bfloat16)

    nt = (((1,), (1,)), ((), ()))

    def products(q, g, first, last):
        rows = pl.ds(first * OWN[q], (last - first) * OWN[q])
        rows_a = a_all[step(x, ring[g], 4)].reshape(2 * a_all.shape[2], -1)
        cs[q][g, rows] = lax.dot_general(
            v_one[q][rows, :], rows_a, nt, preferred_element_type=jnp.float32
        ) - lax.dot_general(v_two[q][rows, :], rows_a, nt, preferred_element_type=jnp.float32)

    def part_of(q, t, g):
        j = targets.index(4 if t == -4 else t)
        return cs[q][g, pl.ds(j * OWN[q], OWN[q]), :]

    def streams(g):
        return ((1, 0, 3 + g % 2), (-1, 1, 4 - g % 2))

    def hop(q, g, i, s, d):
        to = dev(x, y, c, step(z, d, 8))
        return (
            remote(sq[q].at[g, i, s], rq[q].at[g, i, s], rq_s.at[q, g, i, s], rq_r.at[q, g, i, s], to),
            remote(ss.at[q, g, i, s], rs.at[q, g, i, s], rs_s.at[q, g, i, s], rs_r.at[q, g, i, s], to),
        )

    def incoming(q, g, i, s, d):
        for cp in hop(q, g, i, s, d):
            cp.wait_recv()
        return dequantize(rq[q][g, i, s], rs[q, g, i, s])

    def advance(q, s, *groups):
        for g in groups:
            for d, i, length in streams(g):
                if s < length:
                    val = part_of(q, d * (length - s), g)
                    if s:
                        val = val + incoming(q, g, i, s - 1, d)
                    quantize(val, sq[q].at[g, i, s], ss.at[q, g, i, s])
                    for cp in hop(q, g, i, s, d):
                        cp.start()

    o_mine = xor3(z, kappa)
    end = jnp.where(z > o_mine, 1, 0)

    def deliver(q, g, dc, mirror):
        xx, cc = step(x, ring[g], 4), step(c, dc, 2)
        lanes = pl.ds(pl.multiple_of(128 * cc, 128), 256)
        slot = 2 * (z if mirror else o_mine) + end
        n, m = g * 2 + dc, int(mirror)
        to = dev(xx, y, cc, o_mine if mirror else z)
        if not (g or dc or mirror):
            return (
                pltpu.make_async_copy(fq[q].at[g, :, lanes], gq[q].at[slot], own_s.at[1, q]),
                pltpu.make_async_copy(fs.at[q, g], gs.at[q, slot], own_s.at[2, q]),
            )
        return (
            remote(fq[q].at[g, :, lanes], gq[q].at[slot], fq_s.at[q, m, n], fq_r.at[q, m, kappa], to),
            remote(fs.at[q, g], gs.at[q, slot], fs_s.at[q, m, n], fs_r.at[q, m, kappa], to),
        )

    def finish(q, *groups):
        for g in groups:
            val = part_of(q, 0, g)
            for d, i, length in streams(g):
                val = val + incoming(q, g, i, length - 1, d)
            quantize(val, fq[q].at[g], fs.at[q, g])

            @pl.when(kappa > 0)
            def _():
                for dc in (0, 1):
                    for cp in deliver(q, g, dc, True):
                        cp.start()

            for dc in (0, 1):
                for cp in deliver(q, g, dc, False):
                    cp.start()

    def arrived(q, m, k):
        remote(fq[q].at[0, :, pl.ds(0, 256)], gq[q].at[0], fq_s.at[q, 0, 0], fq_r.at[q, m, k], other).wait_recv()
        remote(fs.at[q, 0], gs.at[q, 0], fs_s.at[q, 0, 0], fs_r.at[q, m, k], other).wait_recv()

    tn = (((0,), (0,)), ((), ()))

    def assemble(q):
        for dx in (0, 3, 1, 2):
            for dc in range(2):
                k = kid(step(x, dx, 4), step(c, dc, 2))
                if dx or dc:
                    arrived(q, 0, k)
                else:
                    for cp in deliver(q, 0, 0, False):
                        cp.wait()

                @pl.when(k > 0)
                def _():
                    arrived(q, 1, k)

        full = jnp.concatenate([dequantize(gq[q][i], gs[q, i]) for i in range(16)], axis=0)
        top = full.astype(jnp.bfloat16)
        low = (full - top.astype(jnp.float32)).astype(jnp.bfloat16)
        w_rows = w_ref[pl.ds(16 * OWN[0] * q, 16 * OWN[q]), :]
        return lax.dot_general(top, w_rows, tn, preferred_element_type=jnp.float32) + lax.dot_general(
            low, w_rows, tn, preferred_element_type=jnp.float32
        )

    spread(0)
    for cp in inputs[3:]:
        cp.wait()
    table = table_ref[z]
    sign = table[3:4].astype(jnp.float32)

    @pl.loop(0, 9)
    def _(i):
        rows = lax.broadcasted_iota(jnp.int32, (128, 8 * G * G), 0) + i * 128
        hit = rows == table[0:1]
        w_ref[pl.ds(pl.multiple_of(i * 128, 128), 128), :] = jnp.where(hit, sign, 0.0).astype(jnp.bfloat16)

    vir, occ = column(vir_ref[...]), column(occ_ref[...])
    ev_ref[...] = looked_up(table[1:2], vir) + looked_up(table[2:3], vir)
    ep_ref[...] = column(looked_up(pairs_ref[0:1], occ) + looked_up(pairs_ref[1:2], occ))
    for q in range(2):
        gq[q][2 * z + 1] = jnp.zeros(gq[q].shape[1:], gq[q].dtype)
        gs[q, 2 * z + 1] = jnp.zeros(gs.shape[2:], gs.dtype)

    pass_on(0)
    spread(1)
    pass_on_a()
    other_core(0, 0)
    gathered(0)
    select(0, 0, 3)
    products(0, 0, 0, 3)
    advance(0, 0, 0)
    share_near()
    select(0, 3, 8)
    products(0, 0, 3, 8)
    pass_on(1)
    advance(0, 1, 0)
    other_core(2, 1)
    products(0, 1, 0, 8)
    advance(0, 0, 1)
    other_core(1, -1)
    products(0, 2, 0, 8)
    advance(0, 0, 2)
    advance(0, 2, 0)
    share_far()
    advance(0, 1, 1, 2)
    advance(0, 3, 0)
    other_core(3, 2)
    products(0, 3, 0, 8)
    advance(0, 0, 3)
    finish(0, 0)
    advance(0, 2, 1, 2)
    gathered(1)
    select(1, 0, 8)
    products(1, 0, 0, 8)
    products(1, 1, 0, 8)
    advance(1, 0, 0, 1)
    advance(0, 1, 3)
    advance(0, 3, 1, 2)
    products(1, 2, 0, 8)
    products(1, 3, 0, 8)
    advance(1, 0, 2, 3)
    finish(0, 1, 2)
    advance(0, 2, 3)
    advance(1, 1, 0, 1, 2, 3)
    advance(0, 3, 3)
    advance(1, 2, 0, 1, 2, 3)
    finish(0, 3)
    advance(1, 3, 0, 1, 2, 3)
    finish(1, 0, 1, 2, 3)
    o_ref[...] = assemble(0)
    o_ref[...] = o_ref[...] + assemble(1)
    leaving = []
    for i in range(3):
        rows = pl.ds(64 * i, 64)
        out_ref[rows, :] = o_ref[pl.ds(pl.multiple_of(64 * (c + i), 8), 64), :] / (ep_ref[rows, :] - ev_ref[...])
        leaving.append(pltpu.make_async_copy(out_ref.at[rows], out_hbm.at[rows], out_s.at[i]))
        leaving[-1].start()

    for q in range(2):
        for n in range(8):
            blk = v_buf[q].at[0, 0]
            if n:
                remote(blk, blk, vx_s.at[q, n], vx_r.at[q, 0], other).wait_send()
            for di in range(2):
                remote(blk, blk, vy_s.at[q, di, n], vx_r.at[q, 0], other).wait_send()
            remote(blk, blk, vf_s.at[q, n], vx_r.at[q, 0], other).wait_send()
    half_a = a_all.at[0, 0, pl.ds(0, 96)]
    for di in range(2):
        for h in range(2):
            remote(half_a, half_a, ax_s.at[di, h], ax_r.at[di, h], other).wait_send()
        remote(half_a, half_a, af_s.at[di], af_r.at[di], other).wait_send()
    for n in range(4):
        remote(a_ref, a_ref, ap_s.at[n], ap_r.at[n], other).wait_send()
    for q in range(2):
        for g in range(4):
            for d, i, length in streams(g):
                for s in range(length):
                    for cp in hop(q, g, i, s, d):
                        cp.wait_send()
            for dc in (0, 1):
                if g or dc:
                    for cp in deliver(q, g, dc, False):
                        cp.wait_send()

    @pl.when(kappa > 0)
    def _():
        for q in range(2):
            for g in range(4):
                for dc in (0, 1):
                    for cp in deliver(q, g, dc, True):
                        cp.wait_send()

    for cp in leaving:
        cp.wait()


def on_device(amplitudes, integrals, pair_index, eps_occ, eps_vir):
    rows, depth = amplitudes.shape
    f32, bf16, i16 = jnp.float32, jnp.bfloat16, jnp.int16
    dma = pltpu.SemaphoreType.DMA
    sel0, sel1 = [jnp.asarray(s, bf16) for s in selection_tables()]
    order, table = jnp.asarray(row_order(), bf16), jnp.asarray(output_tables())
    vt, pairs, occ, vir = integrals.T, pair_index.T, eps_occ.reshape(1, -1), eps_vir.reshape(1, -1)

    def both(shape, dtype):
        return [pltpu.VMEM(shape(BLOCK[q], OWN[q]), dtype) for q in range(2)]

    return pl.pallas_call(
        kernel,
        out_shape=jax.ShapeDtypeStruct((rows, 8 * G * G), f32),
        in_specs=[pl.BlockSpec(memory_space=pl.ANY)] * 9,
        out_specs=pl.BlockSpec(memory_space=pl.ANY),
        scratch_shapes=[
            *[pltpu.VMEM(a.shape, a.dtype) for a in (sel0, sel1, order, table, vt, pairs, occ, vir)],
            dma((9,)),
            dma((3,)),
            pltpu.VMEM((rows, 8 * G * G), f32),
            pltpu.VMEM((4, 2, rows, depth), bf16),
            pltpu.VMEM((8 * G * G, 8 * G * G), bf16),
            pltpu.VMEM((256, 8 * G * G), f32),
            pltpu.VMEM((rows, 1), f32),
            pltpu.VMEM((1, 8 * G * G), f32),
            *both(lambda b, n: (8, b, depth), bf16),
            *both(lambda b, n: (8, 4, b, depth), bf16),
            *both(lambda b, n: (8 * n, depth), bf16),
            *both(lambda b, n: (8 * n, depth), bf16),
            *both(lambda b, n: (4, 8 * n, 2 * rows), f32),
            *both(lambda b, n: (4, 2, 4, n, 2 * rows), i16),
            *both(lambda b, n: (4, 2, 4, n, 2 * rows), i16),
            *both(lambda b, n: (4, n, 2 * rows), i16),
            *both(lambda b, n: (16, n, 256), i16),
            pltpu.VMEM((2, 4, 2, 4, 8, 128), bf16),
            pltpu.VMEM((2, 4, 2, 4, 8, 128), bf16),
            pltpu.VMEM((2, 4, 8, 128), bf16),
            pltpu.VMEM((2, 16, 8, 128), bf16),
            dma((2, 8)), dma((2, 8)), dma((2, 2, 8)), dma((2, 2, 8)), dma((2, 8)), dma((2, 8)),
            dma((2, 2)), dma((2, 2)), dma((2,)), dma((2,)), dma((4,)), dma((4,)), dma((3, 2)),
            dma((2, 4, 2, 4)), dma((2, 4, 2, 4)), dma((2, 4, 2, 4)), dma((2, 4, 2, 4)),
            dma((2, 2, 8)), dma((2, 2, 8)), dma((2, 2, 8)), dma((2, 2, 8)),
        ],
        compiler_params=pltpu.CompilerParams(
            collective_id=0, has_side_effects=True, vmem_limit_bytes=60 * 1024 * 1024
        ),
    )(sel0, sel1, order, table, amplitudes, vt, pairs, occ, vir)


def solution(mesh):
    in_specs = (P("pair", "slab"), P("slab", "pair"), P("pair", None), P(), P())
    return jax.shard_map(on_device, mesh=mesh, in_specs=in_specs, out_specs=P("pair", "slab"), check_vma=False)
```

time: 248 us -> 80.2 us (0.32)
  waiting for transfers between devices: 177 us -> 0 us
  Pallas kernels: 0 us -> 77.9 us
  local copies, waits for them, and re-layouts: 29 us -> 2.14 us
  other arithmetic: 14.8 us -> 0 us
  between operations: 13.5 us -> 0.01 us
  matrix products: 13.1 us -> 0 us
    all_gather x1 -> x0, waiting for transfers between devices: 94.7 us -> none  [on_device(): lax.all_gather(integrals, 'pair', axis=1, tiled=True)]
    reduce_scatter x1 -> x0, waiting for transfers between devices: 81.3 us -> none  [on_device(): summed = lax.psum_scatter(antisym, 'slab', scatter_dimension=1, tiled=True)]
    pallas_call x0 -> x1, Pallas kernels: none -> 77.9 us  [on_device(): pl.pallas_call(kernel, out_shape=jax.ShapeDtypeStruct((rows, 8 * G * G),...]
    reshape x3 -> x0, local copies, waits for them, and re-layouts: 29 us -> none  [the longest x2 18.9 us: on_device(): ladder_cube = ladder.reshape(num_pairs, vir_count, vir_count)]
    dot_general x1 -> x0, matrix products: 13.1 us -> none  [on_device(): jnp.dot(amplitudes, lax.all_gather(integrals, 'pair', axis=1, tiled=True)...]
    sub x1 -> x0, other arithmetic: 12.2 us -> none  [on_device(): ladder_cube - jnp.swapaxes(ladder_cube, 1, 2)]
  transfers between devices with their start and end apart: 2 -> 0, of which waited for: 2 -> 0; matrix products, arithmetic and copies ran while one was open for 0% -> 0% of each run, Pallas kernels for 0% -> 0%
where the time goes in v1:
time: 80.2 us; the launch traced here: 80 us
  Pallas kernels  77.9 us (97%)
  local copies, waits for them, and re-layouts  2.14 us (3%)
    pallas_call x1, Pallas kernels, on_device(): pl.pallas_call(kernel, out_shape=jax.ShapeDtypeStruct((rows, 8 * G * G),...  77.9 us
    unnamed x1, local copies, waits for them, and re-layouts  2.14 us

profile of v1, /device:TPU:1, one launch (start us, length us, event | category | flops | bytes accessed | tf_op | source)
XLA Modules:
  0.0 80.0 jit_solution(192397457386828801)
XLA Ops:
  0.0 77.9 %shard_map.91 = f32[192,1152]{1,0:T(8,128)} custom-call(bf16[3,2,48,96]{3,2,1,0:T(8,128)(2,1)} %constant.8.clone.sel0_hbm, bf16[3,2,24,64]{3,2,1,0:T(8,128)(2,1)} %constant.9.clone.sel1_hbm, bf16[320,288]{1,0:T(8,128)(2,1)} %constant.10.clone.order_hbm, s32[8,4,1152]{2,1,0:T(4,128)} %constant.11.clone.table_hbm, bf16[192,1152]{1,0:T(8,128)(2,1)} %a_hbm.1, ...), custom_call_target="tpu_custom_call" | custom-call | tf_op jit(solution)/shard_map/pallas_call | solution.py:506
  77.9 2.1 %copy.11 = f32[192,1152]{1,0:T(8,128)} copy(f32[192,1152]{1,0:T(8,128)} %shard_map.91) | data formatting | bytes 1769472

commit v2 on v1

--- a/solution.py
+++ b/solution.py
@@ -10,24 +10,24 @@
 
 MESH = pl.DeviceIdType.MESH
 G = 12
-BLOCK = (24, 16)
-OWN = (48, 24)
+BLOCK = (16, 24)
+OWN = (24, 48)
 QMAX = 32767.0
 
 
 def chunk_of(u, v):
-    return 0 if (u + v) % 3 else 1
+    return 1 if (u + v) % 3 else 0
 
 
 def block_row(u, v):
     q = chunk_of(u, v)
     rank = sum(chunk_of(u, i) == q for i in range(v))
-    return BLOCK[q] * (u // 3) + (8, 4)[q] * (u % 3) + rank
+    return BLOCK[q] * (u // 3) + (4, 8)[q] * (u % 3) + rank
 
 
 def own_row(i, v):
     q = chunk_of(i, v)
-    return (8, 4)[q] * i + sum(chunk_of(i, j) == q for j in range(v))
+    return (4, 8)[q] * i + sum(chunk_of(i, j) == q for j in range(v))
 
 
 def selection_tables():
@@ -381,6 +381,8 @@
         )
 
     spread(0)
+    pass_on(0)
+    spread(1)
     for cp in inputs[3:]:
         cp.wait()
     table = table_ref[z]
@@ -399,52 +401,57 @@
         gq[q][2 * z + 1] = jnp.zeros(gq[q].shape[1:], gq[q].dtype)
         gs[q, 2 * z + 1] = jnp.zeros(gs.shape[2:], gs.dtype)
 
-    pass_on(0)
-    spread(1)
     pass_on_a()
     other_core(0, 0)
     gathered(0)
-    select(0, 0, 3)
-    products(0, 0, 0, 3)
+    select(0, 0, 8)
+    products(0, 0, 0, 8)
     advance(0, 0, 0)
     share_near()
-    select(0, 3, 8)
-    products(0, 0, 3, 8)
     pass_on(1)
-    advance(0, 1, 0)
     other_core(2, 1)
     products(0, 1, 0, 8)
     advance(0, 0, 1)
     other_core(1, -1)
     products(0, 2, 0, 8)
     advance(0, 0, 2)
-    advance(0, 2, 0)
+    advance(0, 1, 0)
     share_far()
     advance(0, 1, 1, 2)
-    advance(0, 3, 0)
+    advance(0, 2, 0)
     other_core(3, 2)
     products(0, 3, 0, 8)
     advance(0, 0, 3)
-    finish(0, 0)
     advance(0, 2, 1, 2)
+    advance(0, 3, 0)
     gathered(1)
-    select(1, 0, 8)
-    products(1, 0, 0, 8)
-    products(1, 1, 0, 8)
-    advance(1, 0, 0, 1)
+    select(1, 0, 3)
+    products(1, 0, 0, 3)
+    advance(1, 0, 0)
+    products(1, 1, 0, 3)
+    advance(1, 0, 1)
     advance(0, 1, 3)
     advance(0, 3, 1, 2)
-    products(1, 2, 0, 8)
-    products(1, 3, 0, 8)
-    advance(1, 0, 2, 3)
-    finish(0, 1, 2)
+    products(1, 2, 0, 3)
+    advance(1, 0, 2)
+    products(1, 3, 0, 3)
+    advance(1, 0, 3)
+    select(1, 3, 8)
+    products(1, 0, 3, 8)
+    products(1, 1, 3, 8)
+    advance(1, 1, 0, 1)
     advance(0, 2, 3)
-    advance(1, 1, 0, 1, 2, 3)
+    products(1, 2, 3, 8)
+    products(1, 3, 3, 8)
+    advance(1, 1, 2, 3)
+    finish(0, 0, 1, 2)
+    advance(1, 2, 0, 1)
     advance(0, 3, 3)
-    advance(1, 2, 0, 1, 2, 3)
+    advance(1, 2, 2, 3)
+    advance(1, 3, 0, 1)
     finish(0, 3)
-    advance(1, 3, 0, 1, 2, 3)
-    finish(1, 0, 1, 2, 3)
+    advance(1, 3, 2, 3)
+    finish(1, 3, 1, 2, 0)
     o_ref[...] = assemble(0)
     o_ref[...] = o_ref[...] + assemble(1)
     leaving = []

time: 80.2 us -> 78.5 us (0.979)
  Pallas kernels: 77.9 us -> 76.3 us
    pallas_call x1, Pallas kernels: 77.9 us -> 76.3 us  [on_device(): pl.pallas_call(kernel, out_shape=jax.ShapeDtypeStruct((rows, 8 * G * G),...]
where the time goes in v2:
time: 78.5 us; the launch traced here: 78.4 us
  Pallas kernels  76.3 us (97%)
  local copies, waits for them, and re-layouts  2.14 us (3%)
    pallas_call x1, Pallas kernels, on_device(): pl.pallas_call(kernel, out_shape=jax.ShapeDtypeStruct((rows, 8 * G * G),...  76.3 us
    unnamed x1, local copies, waits for them, and re-layouts  2.14 us

profile of v2, /device:TPU:1, one launch (start us, length us, event | category | flops | bytes accessed | tf_op | source)
XLA Modules:
  0.0 78.4 jit_solution(15226963358230791035)
XLA Ops:
  0.0 76.3 %shard_map.91 = f32[192,1152]{1,0:T(8,128)} custom-call(bf16[3,2,24,64]{3,2,1,0:T(8,128)(2,1)} %constant.8.clone.sel0_hbm, bf16[3,2,48,96]{3,2,1,0:T(8,128)(2,1)} %constant.9.clone.sel1_hbm, bf16[320,288]{1,0:T(8,128)(2,1)} %constant.10.clone.order_hbm, s32[8,4,1152]{2,1,0:T(4,128)} %constant.11.clone.table_hbm, bf16[192,1152]{1,0:T(8,128)(2,1)} %a_hbm.1, ...), custom_call_target="tpu_custom_call" | custom-call | tf_op jit(solution)/shard_map/pallas_call | solution.py:513
  76.3 2.1 %copy.11 = f32[192,1152]{1,0:T(8,128)} copy(f32[192,1152]{1,0:T(8,128)} %shard_map.91) | data formatting | bytes 1769472
